TPU v7x, 32 devices: a whole 2x2x4 slice. The times are simulated.
32 devices in a mesh: groups: 2 (over y), seq: 4 (over z), rep: 2 (over x), fsdp: 2 (over core).
Axes of the slice: x: 2, y: 2, z: 4, core: 2. Of those that a mesh axis runs over, the one named last changes fastest.
Arguments:
- activations: bfloat16 [8, 512, 2048], P(('groups', 'rep', 'fsdp'), 'seq'), parts along dimension 0, may hold values from -6 to 6
- queries: bfloat16 [8, 512, 2048], P(('groups', 'rep', 'fsdp'), 'seq'), parts along dimension 0, may hold values from -102 to 102
- key_weight: bfloat16 [2048, 512], P(('seq', 'fsdp')), may hold values from -0.125 to 0.125
- value_weight: bfloat16 [2048, 512], P(('seq', 'fsdp')), may hold values from -0.125 to 0.125
- segment_ids: int32 [8, 512], P(('groups', 'rep', 'fsdp'), 'seq'), parts along dimension 0, may hold values from 0 to 3, never falling along the last dimension, each value on 1 to 384 neighbouring positions
- out_grad: bfloat16 [8, 512, 2048], P(('groups', 'rep', 'fsdp'), 'seq'), parts along dimension 0, may hold values from -6 to 6
Outputs:
- context: bfloat16 [8, 512, 2048], P(('groups', 'rep', 'fsdp'), 'seq'), parts along dimension 0
- query_grad: bfloat16 [8, 512, 2048], P(('groups', 'rep', 'fsdp'), 'seq'), parts along dimension 0
- input_grad: bfloat16 [8, 512, 2048], P(('groups', 'rep', 'fsdp'), 'seq'), parts along dimension 0
- key_weight_grad: bfloat16 [4096, 512], P(('groups', 'seq', 'fsdp')), parts along dimension 0
- value_weight_grad: bfloat16 [4096, 512], P(('groups', 'seq', 'fsdp')), parts along dimension 0
There are 2 independent parts, one for each index of `groups`. A program takes and returns all parts, laid end to end along the dimension named above; an argument that names none is the same for every part. Nothing has to cross between parts.
Inputs may be any that keep to these rules, and one draw needn't show every extreme that they name: `segment_ids`: document numbers never fall along a sequence; a document covers at most 384 positions.
All inputs are finite; a program needn't handle non-finite values.
Results may differ from a plain program's by a relative error of at most 0.025.
The roundings to bfloat16 on the way count: a program that leaves them out, or rounds other values in their place, can miss the bound.
Values may be sent and summed in bfloat16 or wider, within the bound.
No kernel may reach another device: no remote copies, remote signals or barrier semaphores. Data moves between devices by JAX's collectives and lax.ppermute only.
A program may use at most 64 MiB of HBM per device.

v0:
```python
import math
import jax
import jax.numpy as jnp
from jax import lax
from jax.sharding import PartitionSpec as P

HEADS = 16
KV_HEADS = 4
HEAD_DIM = 128
masked_low = -1e30


def block_mask(seg_all, row_start, col_start, block_width):
    row_pos = row_start + lax.iota(jnp.int32, block_width)
    col_pos = col_start + lax.iota(jnp.int32, block_width)
    seg_rows = lax.dynamic_slice_in_dim(seg_all, row_start, block_width)
    seg_cols = lax.dynamic_slice_in_dim(seg_all, col_start, block_width)
    return (col_pos[None, :] <= row_pos[:, None]) & (seg_cols[None, :] == seg_rows[:, None])


def block_scores(query_block, key_block, inv_root):
    return (
        jnp.einsum("qhd,khd->hqk", query_block, key_block, preferred_element_type=jnp.float32)
        * inv_root
    )


def take_block(source, index, block_width):
    return lax.dynamic_slice_in_dim(source, index * block_width, block_width, 0)


def attend(query_part, key_part, value_part, seg_all):
    length, heads_here, head_size = query_part.shape
    block_width = min(512, length)
    block_count = length // block_width
    inv_root = 1.0 / math.sqrt(head_size)

    def stats_row(i, log_totals):
        query_block = take_block(query_part, i, block_width)

        def stats_inner(j, state_now):
            running_max, running_sum = state_now
            scores = block_scores(query_block, take_block(key_part, j, block_width), inv_root)
            allowed = block_mask(seg_all, i * block_width, j * block_width, block_width)[None]
            scores = jnp.where(allowed, scores, masked_low)
            new_max = jnp.maximum(running_max, jnp.max(scores, axis=-1))
            weights = jnp.where(allowed, jnp.exp(scores - new_max[..., None]), 0.0)
            running_sum = running_sum * jnp.exp(running_max - new_max) + jnp.sum(weights, axis=-1)
            return (new_max, running_sum)

        start_state = (
            jnp.full((heads_here, block_width), masked_low, jnp.float32),
            jnp.zeros((heads_here, block_width), jnp.float32),
        )
        running_max, running_sum = lax.fori_loop(0, i + 1, stats_inner, start_state)
        return lax.dynamic_update_slice_in_dim(
            log_totals, running_max + jnp.log(running_sum), i * block_width, 1
        )

    log_totals = lax.fori_loop(
        0, block_count, stats_row, jnp.zeros((heads_here, length), jnp.float32)
    )

    def out_row(i, out_all):
        query_block = take_block(query_part, i, block_width)
        log_block = lax.dynamic_slice_in_dim(log_totals, i * block_width, block_width, 1)

        def out_inner(j, accum_out):
            scores = block_scores(query_block, take_block(key_part, j, block_width), inv_root)
            allowed = block_mask(seg_all, i * block_width, j * block_width, block_width)[None]
            probs_low = jnp.where(allowed, jnp.exp(scores - log_block[..., None]), 0.0).astype(
                jnp.bfloat16
            )
            return accum_out + jnp.einsum(
                "hqk,khd->qhd",
                probs_low,
                take_block(value_part, j, block_width),
                preferred_element_type=jnp.float32,
            )

        accum_out = lax.fori_loop(
            0, i + 1, out_inner, jnp.zeros((block_width, heads_here, head_size), jnp.float32)
        )
        return lax.dynamic_update_slice_in_dim(
            out_all, accum_out.astype(jnp.bfloat16), i * block_width, 0
        )

    out_all = lax.fori_loop(
        0, block_count, out_row, jnp.zeros((length, heads_here, head_size), jnp.bfloat16)
    )
    return (out_all, log_totals)


def attend_grads(query_part, key_part, value_part, seg_all, out_part, log_totals, grad_part):
    length, heads_here, head_size = query_part.shape
    block_width = min(512, length)
    block_count = length // block_width
    inv_root = 1.0 / math.sqrt(head_size)
    row_dots = jnp.einsum("qhd,qhd->hq", grad_part, out_part, preferred_element_type=jnp.float32)

    def grad_row(i, state_now):
        query_all, key_all, value_all = state_now
        query_block = take_block(query_part, i, block_width)
        grad_block = take_block(grad_part, i, block_width)
        log_block = lax.dynamic_slice_in_dim(log_totals, i * block_width, block_width, 1)
        dots_block = lax.dynamic_slice_in_dim(row_dots, i * block_width, block_width, 1)

        def grad_inner(j, inner_state):
            query_accum, key_accum, value_accum = inner_state
            key_block = take_block(key_part, j, block_width)
            value_block = take_block(value_part, j, block_width)
            scores = block_scores(query_block, key_block, inv_root)
            allowed = block_mask(seg_all, i * block_width, j * block_width, block_width)[None]
            probs = jnp.where(allowed, jnp.exp(scores - log_block[..., None]), 0.0)
            probs_low = probs.astype(jnp.bfloat16)
            value_new = take_block(value_accum, j, block_width) + jnp.einsum(
                "hqk,qhd->khd", probs_low, grad_block, preferred_element_type=jnp.float32
            )
            value_accum = lax.dynamic_update_slice_in_dim(
                value_accum, value_new, j * block_width, 0
            )
            prob_grad = jnp.einsum(
                "qhd,khd->hqk", grad_block, value_block, preferred_element_type=jnp.float32
            )
            score_grad = (probs * (prob_grad - dots_block[..., None])).astype(jnp.bfloat16)
            query_accum = query_accum + jnp.einsum(
                "hqk,khd->qhd", score_grad, key_block, preferred_element_type=jnp.float32
            )
            key_new = take_block(key_accum, j, block_width) + jnp.einsum(
                "hqk,qhd->khd", score_grad, query_block, preferred_element_type=jnp.float32
            )
            key_accum = lax.dynamic_update_slice_in_dim(key_accum, key_new, j * block_width, 0)
            return (query_accum, key_accum, value_accum)

        start_state = (
            jnp.zeros((block_width, heads_here, head_size), jnp.float32),
            key_all,
            value_all,
        )
        query_accum, key_all, value_all = lax.fori_loop(0, i + 1, grad_inner, start_state)
        query_all = lax.dynamic_update_slice_in_dim(
            query_all, (query_accum * inv_root).astype(jnp.bfloat16), i * block_width, 0
        )
        return (query_all, key_all, value_all)

    zero_grads = jnp.zeros((length, heads_here, head_size), jnp.float32)
    start_all = (jnp.zeros((length, heads_here, head_size), jnp.bfloat16), zero_grads, zero_grads)
    query_all, key_all, value_all = lax.fori_loop(0, block_count, grad_row, start_all)
    return (query_all, (key_all * inv_root).astype(jnp.bfloat16), value_all.astype(jnp.bfloat16))


def body(activations, queries, key_weight, value_weight, segment_ids, out_grad):
    rows_here = activations.shape[1]
    inputs = activations[0]
    kv_width = key_weight.shape[1]
    seq_devices = lax.axis_size("seq")
    heads_here = HEADS // seq_devices
    kv_group = HEADS // KV_HEADS
    stacked = jnp.concatenate([key_weight, value_weight], axis=1)
    columns = inputs
    projected = jnp.dot(
        columns,
        lax.all_gather(stacked, ("seq", "fsdp"), axis=0, tiled=True),
        preferred_element_type=jnp.float32,
    )
    projected = projected.astype(jnp.bfloat16)
    key_rows = projected[:, :kv_width].reshape(rows_here, KV_HEADS, HEAD_DIM)
    value_rows = projected[:, kv_width:].reshape(rows_here, KV_HEADS, HEAD_DIM)
    kv_copies = max(kv_group // heads_here, 1)
    query_heads = queries[0].reshape(rows_here, HEADS, HEAD_DIM)
    sent = (
        query_heads,
        jnp.repeat(key_rows, kv_copies, axis=1),
        jnp.repeat(value_rows, kv_copies, axis=1),
    )
    query_part, key_part, value_part = (
        lax.all_to_all(sent[0], "seq", split_axis=1, concat_axis=0, tiled=True),
        lax.all_to_all(sent[1], "seq", split_axis=1, concat_axis=0, tiled=True),
        lax.all_to_all(sent[2], "seq", split_axis=1, concat_axis=0, tiled=True),
    )
    widen_by = heads_here // key_part.shape[1]
    key_part = jnp.repeat(key_part, widen_by, axis=1)
    value_part = jnp.repeat(value_part, widen_by, axis=1)
    seg_all = lax.all_gather(segment_ids[0], "seq", axis=0, tiled=True)
    out_part, log_totals = attend(query_part, key_part, value_part, seg_all)
    context = lax.all_to_all(out_part, "seq", split_axis=0, concat_axis=1, tiled=True).reshape(
        1, rows_here, HEADS * HEAD_DIM
    )
    grad_part = lax.all_to_all(
        out_grad[0].reshape(rows_here, HEADS, HEAD_DIM),
        "seq",
        split_axis=1,
        concat_axis=0,
        tiled=True,
    )
    query_back, key_back, value_back = attend_grads(
        query_part, key_part, value_part, seg_all, out_part, log_totals, grad_part
    )
    query_tok, key_tok, value_tok = (
        lax.all_to_all(query_back, "seq", split_axis=0, concat_axis=1, tiled=True),
        lax.all_to_all(key_back, "seq", split_axis=0, concat_axis=1, tiled=True),
        lax.all_to_all(value_back, "seq", split_axis=0, concat_axis=1, tiled=True),
    )
    key_sum = (
        key_tok.reshape(rows_here, KV_HEADS, kv_group, HEAD_DIM).astype(jnp.float32).sum(axis=2)
    )
    value_sum = (
        value_tok.reshape(rows_here, KV_HEADS, kv_group, HEAD_DIM).astype(jnp.float32).sum(axis=2)
    )
    grad_kv = jnp.concatenate(
        [
            key_sum.astype(jnp.bfloat16).reshape(rows_here, kv_width),
            value_sum.astype(jnp.bfloat16).reshape(rows_here, kv_width),
        ],
        axis=1,
    )
    input_grad = lax.dot_general(
        grad_kv,
        lax.all_gather(stacked, ("seq", "fsdp"), axis=0, tiled=True),
        (((1,), (1,)), ((), ())),
        preferred_element_type=jnp.float32,
    )
    input_grad = input_grad.astype(jnp.bfloat16).reshape(1, rows_here, inputs.shape[1])
    columns = inputs
    grad_shard = lax.psum_scatter(
        lax.dot_general(
            columns, grad_kv, (((0,), (0,)), ((), ())), preferred_element_type=jnp.float32
        ).astype(jnp.bfloat16),
        ("seq", "fsdp"),
        scatter_dimension=0,
        tiled=True,
    ).astype(jnp.float32)
    grad_total = lax.psum(grad_shard, "rep").astype(jnp.bfloat16)
    query_grad = query_tok.reshape(1, rows_here, HEADS * HEAD_DIM)
    return (context, query_grad, input_grad, grad_total[:, :kv_width], grad_total[:, kv_width:])


def solution(mesh):
    return jax.shard_map(
        body,
        mesh=mesh,
        in_specs=(
            P(("groups", "rep", "fsdp"), "seq", None),
            P(("groups", "rep", "fsdp"), "seq", None),
            P(("seq", "fsdp"), None),
            P(("seq", "fsdp"), None),
            P(("groups", "rep", "fsdp"), "seq"),
            P(("groups", "rep", "fsdp"), "seq", None),
        ),
        out_specs=(
            P(("groups", "rep", "fsdp"), "seq", None),
            P(("groups", "rep", "fsdp"), "seq", None),
            P(("groups", "rep", "fsdp"), "seq", None),
            P(("groups", "seq", "fsdp"), None),
            P(("groups", "seq", "fsdp"), None),
        ),
        check_vma=False,
    )
```

profile of v0, /device:TPU:0, one launch (start us, length us, event | category | flops | bytes accessed | tf_op | source)
XLA Modules:
  0.0 248.5 jit_solution(1533762481953320926)
XLA Ops:
  7.2 1.9 pad_maximum_fusion
  9.2 2.0 copy.45
  11.2 6.3 %all-to-all-start.1 = ((bf16[128,16,128]{0,2,1:T(8,128)(2,1)}), bf16[128,16,128]{0,2,1:T(8,128)(2,1)S(1)}, u32[]{:S(2)}, u32[]{:S(2)}) async-start(bf16[128,16,128]{0,2,1:T(8,128)(2,1)} %bitcast.9), calls=%async_computation.1 | async-start | bytes 1048576 | tf_op jit(solution)/shard_map/all_to_all | solution.py:177
  17.5 2.0 copy.52
  19.6 24.7 %all-to-all-done.1 = bf16[128,16,128]{0,2,1:T(8,128)(2,1)S(1)} async-done(((bf16[128,16,128]{0,2,1:T(8,128)(2,1)}), bf16[128,16,128]{0,2,1:T(8,128)(2,1)S(1)}, u32[]{:S(2)}, u32[]{:S(2)}) %all-to-all-start.1) | async-done | bytes 524320 | tf_op jit(solution)/shard_map/all_to_all | solution.py:177
  44.2 3.6 %all-to-all-start.4 = ((bf16[128,16,128]{0,2,1:T(8,128)(2,1)}), bf16[128,16,128]{0,2,1:T(8,128)(2,1)S(1)}, u32[]{:S(2)}, u32[]{:S(2)}) async-start(bf16[128,16,128]{0,2,1:T(8,128)(2,1)} %bitcast.22), calls=%async_computation.4 | async-start | bytes 1048576 | tf_op jit(solution)/shard_map/all_to_all | solution.py:189
  47.9 21.7 %all-gather = s32[1,512]{1,0:T(1,128)S(1)} all-gather(s32[1,128]{1,0:T(1,128)S(1)} %copy-done.3), channel_id=2, replica_groups=mesh['groups'=2,'seq'=4,'rep'=2,'fsdp'=2] {'seq'}, dimensions={1}, use_global_device_ids=true | all-gather | bytes 2560 | tf_op jit(solution)/shard_map/all_gather | solution.py:184
  69.5 9.1 %all-gather.3.cloned.1.call-done = bf16[2048,1024]{1,0:T(8,128)(2,1)} async-done(((bf16[256,1024]{1,0:T(8,128)(2,1)}), bf16[2048,1024]{1,0:T(8,128)(2,1)}) %all-gather.3.cloned.1.call-update) | async-done | bytes 4194320 | tf_op jit(solution)/shard_map/all_gather | solution.py:163
  78.7 3.5 %fusion.11 = bf16[128,1024]{0,1:T(8,128)(2,1)S(1)} fusion(bf16[2048,1024]{1,0:T(8,128)(2,1)} %all-gather.3.cloned.1.call-done, bf16[1,128,2048]{2,1,0:T(8,128)(2,1)S(1)} %copy-done), kind=kOutput, calls=%fused_computation.22 | convolution fusion | flops 537001984 | bytes 4980736 | tf_op jit(solution)/shard_map/dot_general | solution.py:161
  83.0 3.3 %all-to-all-start = ((bf16[128,4,128]{2,0,1:T(8,128)(2,1)}), bf16[128,4,128]{2,0,1:T(8,128)(2,1)S(1)}, u32[]{:S(2)}, u32[]{:S(2)}) async-start(bf16[128,4,128]{2,0,1:T(8,128)(2,1)} %copy.44), calls=%async_computation | async-start | bytes 262144 | tf_op jit(solution)/shard_map/all_to_all | solution.py:178
  87.9 4.8 %all-to-all-done = bf16[128,4,128]{2,0,1:T(8,128)(2,1)S(1)} async-done(((bf16[128,4,128]{2,0,1:T(8,128)(2,1)}), bf16[128,4,128]{2,0,1:T(8,128)(2,1)S(1)}, u32[]{:S(2)}, u32[]{:S(2)}) %all-to-all-start) | async-done | bytes 131104 | tf_op jit(solution)/shard_map/all_to_all | solution.py:178
  92.7 3.3 %all-to-all-start.2 = ((bf16[128,4,128]{2,0,1:T(8,128)(2,1)}), bf16[128,4,128]{2,0,1:T(8,128)(2,1)S(1)}, u32[]{:S(2)}, u32[]{:S(2)}) async-start(bf16[128,4,128]{2,0,1:T(8,128)(2,1)} %copy.48), calls=%async_computation.2 | async-start | bytes 262144 | tf_op jit(solution)/shard_map/all_to_all | solution.py:179
  101.9 3.5 %all-to-all-start.7 = ((bf16[512,4,128]{2,1,0:T(4,128)(2,1)}), bf16[512,4,128]{2,1,0:T(4,128)(2,1)S(1)}, u32[]{:S(2)}, u32[]{:S(2)}) async-start(bf16[512,4,128]{2,1,0:T(4,128)(2,1)} %copy.60), calls=%async_computation.7 | async-start | bytes 1048576 | tf_op jit(solution)/shard_map/all_to_all | solution.py:202
  105.4 3.9 %fusion.12 = (f32[4,512]{1,0:T(4,128)S(1)}, bf16[4,512,128]{2,1,0:T(8,128)(2,1)S(1)}) fusion(bf16[4,128,4,128]{3,1,0,2:T(8,128)(2,1)S(1)} %copy.54, bf16[512,128]{1,0:T(8,128)(2,1)S(1)} %bitcast.111, f32[4,512,512]{2,1,0:T(8,128)} %copy-done.1, f32[4,512]{1,0:T(4,128)S(1)} %log_add_fusion, pred[512,512]{0,1:T(8,128)(4,1)S(1)} %fusion.13), kind=kOutput, calls=%fused_computation.24 | convolution fusion | flops 273938432 | bytes 5652480 | tf_op jit(solution)/shard_map/while/body/eval_jaxpr/while/body/hqk,khd->qhd/dot_general | solution.py:74
  113.3 5.2 %all-to-all-done.7 = bf16[512,4,128]{2,1,0:T(4,128)(2,1)S(1)} async-done(((bf16[512,4,128]{2,1,0:T(4,128)(2,1)}), bf16[512,4,128]{2,1,0:T(4,128)(2,1)S(1)}, u32[]{:S(2)}, u32[]{:S(2)}) %all-to-all-start.7) | async-done | bytes 524320 | tf_op jit(solution)/shard_map/all_to_all | solution.py:202
  118.5 3.5 %all-to-all-start.6 = ((bf16[512,4,128]{2,1,0:T(4,128)(2,1)}), bf16[512,4,128]{2,1,0:T(4,128)(2,1)S(1)}, u32[]{:S(2)}, u32[]{:S(2)}) async-start(bf16[512,4,128]{2,1,0:T(4,128)(2,1)} %copy.58), calls=%async_computation.6 | async-start | bytes 1048576 | tf_op jit(solution)/shard_map/all_to_all | solution.py:201
  123.0 12.3 %all-to-all-done.6 = bf16[512,4,128]{2,1,0:T(4,128)(2,1)S(1)} async-done(((bf16[512,4,128]{2,1,0:T(4,128)(2,1)}), bf16[512,4,128]{2,1,0:T(4,128)(2,1)S(1)}, u32[]{:S(2)}, u32[]{:S(2)}) %all-to-all-start.6) | async-done | bytes 524320 | tf_op jit(solution)/shard_map/all_to_all | solution.py:201
  136.1 3.2 %convert_bitcast_fusion = bf16[2048,1024]{0,1:T(8,128)(2,1)} fusion(bf16[1,128,2048]{2,1,0:T(8,128)(2,1)S(1)} %copy-done, bf16[128,512]{0,1:T(8,128)(2,1)S(1)} %bitcast.98, bf16[128,512]{0,1:T(8,128)(2,1)S(1)} %bitcast.100), kind=kOutput, calls=%fused_computation.6 | convolution fusion | flops 539492352 | bytes 4980736 | tf_op jit(solution)/shard_map/dot_general | solution.py:226
  140.6 3.5 %all-to-all-start.3 = ((bf16[512,4,128]{2,1,0:T(4,128)(2,1)}), bf16[512,4,128]{2,1,0:T(4,128)(2,1)S(1)}, u32[]{:S(2)}, u32[]{:S(2)}) async-start(bf16[512,4,128]{2,1,0:T(4,128)(2,1)} %copy.50), calls=%async_computation.3 | async-start | bytes 1048576 | tf_op jit(solution)/shard_map/all_to_all | solution.py:186
  146.2 19.1 %all-to-all-done.3 = bf16[512,4,128]{2,1,0:T(4,128)(2,1)S(1)} async-done(((bf16[512,4,128]{2,1,0:T(4,128)(2,1)}), bf16[512,4,128]{2,1,0:T(4,128)(2,1)S(1)}, u32[]{:S(2)}, u32[]{:S(2)}) %all-to-all-start.3) | async-done | bytes 524320 | tf_op jit(solution)/shard_map/all_to_all | solution.py:186
  165.3 4.3 %all-to-all-start.5 = ((bf16[512,4,128]{2,1,0:T(4,128)(2,1)}), bf16[512,4,128]{2,1,0:T(4,128)(2,1)S(1)}, u32[]{:S(2)}, u32[]{:S(2)}) async-start(bf16[512,4,128]{2,1,0:T(4,128)(2,1)} %copy.56), calls=%async_computation.5 | async-start | bytes 1048576 | tf_op jit(solution)/shard_map/all_to_all | solution.py:200
  169.6 34.6 %reduce-scatter.2.cloned.1.call-done = bf16[256,1024]{0,1:T(8,128)(2,1)} async-done(((bf16[2048,1024]{0,1:T(8,128)(2,1)}), bf16[256,1024]{0,1:T(8,128)(2,1)}) %reduce-scatter.2.cloned.1.call-update) | async-done | bytes 524304 | tf_op jit(solution)/shard_map/reduce_scatter | solution.py:225
  207.0 4.5 %fusion.5 = bf16[1,128,2048]{2,1,0:T(8,128)(2,1)} fusion(bf16[2048,1024]{1,0:T(8,128)(2,1)} %all-gather.3.cloned.1.call-done, bf16[128,512]{0,1:T(8,128)(2,1)S(1)} %bitcast.99, bf16[128,512]{0,1:T(8,128)(2,1)S(1)} %bitcast.101), kind=kOutput, calls=%fused_computation.11 | convolution fusion | flops 537657344 | bytes 4980736 | tf_op jit(solution)/shard_map/dot_general | solution.py:217
  211.5 27.7 %all-reduce.2.cloned.1.call-done = bf16[256,1024]{0,1:T(8,128)(2,1)} async-done(((bf16[256,1024]{0,1:T(8,128)(2,1)}), bf16[256,1024]{0,1:T(8,128)(2,1)}) %all-reduce.2.cloned.1.call-update) | async-done | bytes 524304 | tf_op jit(solution)/shard_map/psum | solution.py:233
  (50 shorter events, 22.9 us)
Async XLA Ops:
  7.2 71.5 %copy-start = (bf16[1,128,2048]{2,1,0:T(8,128)(2,1)S(1)}, bf16[1,128,2048]{2,1,0:T(8,128)(2,1)}, u32[]{:S(2)}) copy-start(bf16[1,128,2048]{2,1,0:T(8,128)(2,1)} %param.6) | copy-start | bytes 1572868
  7.2 40.7 %copy-start.3 = (s32[1,128]{1,0:T(1,128)S(1)}, s32[1,128]{1,0:T(1,128)}, u32[]{:S(2)}) copy-start(s32[1,128]{1,0:T(1,128)} %param.10) | copy-start | bytes 1540
  7.2 71.5 %all-gather.3.cloned.1.call-start = ((), (), s32[]{:S(2)}) async-start(), calls=%async_computation.9 | async-start | bytes 4718592 | tf_op jit(solution)/shard_map/all_gather | solution.py:163
  11.2 33.0 %all-to-all-start.1 = ((bf16[128,16,128]{0,2,1:T(8,128)(2,1)}), bf16[128,16,128]{0,2,1:T(8,128)(2,1)S(1)}, u32[]{:S(2)}, u32[]{:S(2)}) async-start(bf16[128,16,128]{0,2,1:T(8,128)(2,1)} %bitcast.9), calls=%async_computation.1 | async-start | bytes 1048576 | tf_op jit(solution)/shard_map/all_to_all | solution.py:177
  44.2 38.7 %all-to-all-start.4 = ((bf16[128,16,128]{0,2,1:T(8,128)(2,1)}), bf16[128,16,128]{0,2,1:T(8,128)(2,1)S(1)}, u32[]{:S(2)}, u32[]{:S(2)}) async-start(bf16[128,16,128]{0,2,1:T(8,128)(2,1)} %bitcast.22), calls=%async_computation.4 | async-start | bytes 1048576 | tf_op jit(solution)/shard_map/all_to_all | solution.py:189
  83.0 9.7 %all-to-all-start = ((bf16[128,4,128]{2,0,1:T(8,128)(2,1)}), bf16[128,4,128]{2,0,1:T(8,128)(2,1)S(1)}, u32[]{:S(2)}, u32[]{:S(2)}) async-start(bf16[128,4,128]{2,0,1:T(8,128)(2,1)} %copy.44), calls=%async_computation | async-start | bytes 262144 | tf_op jit(solution)/shard_map/all_to_all | solution.py:178
  92.7 9.2 %all-to-all-start.2 = ((bf16[128,4,128]{2,0,1:T(8,128)(2,1)}), bf16[128,4,128]{2,0,1:T(8,128)(2,1)S(1)}, u32[]{:S(2)}, u32[]{:S(2)}) async-start(bf16[128,4,128]{2,0,1:T(8,128)(2,1)} %copy.48), calls=%async_computation.2 | async-start | bytes 262144 | tf_op jit(solution)/shard_map/all_to_all | solution.py:179
  96.9 2.0 copy-start.1
  101.9 16.6 %all-to-all-start.7 = ((bf16[512,4,128]{2,1,0:T(4,128)(2,1)}), bf16[512,4,128]{2,1,0:T(4,128)(2,1)S(1)}, u32[]{:S(2)}, u32[]{:S(2)}) async-start(bf16[512,4,128]{2,1,0:T(4,128)(2,1)} %copy.60), calls=%async_computation.7 | async-start | bytes 1048576 | tf_op jit(solution)/shard_map/all_to_all | solution.py:202
  105.4 3.9 %copy-start.2 = (f32[4,512,512]{2,1,0:T(8,128)S(1)}, f32[4,512,512]{2,1,0:T(8,128)}, u32[]{:S(2)}) copy-start(f32[4,512,512]{2,1,0:T(8,128)} %copy-done.1) | copy-start | bytes 12582916
  110.7 1.4 copy-start.4
  118.5 16.8 %all-to-all-start.6 = ((bf16[512,4,128]{2,1,0:T(4,128)(2,1)}), bf16[512,4,128]{2,1,0:T(4,128)(2,1)S(1)}, u32[]{:S(2)}, u32[]{:S(2)}) async-start(bf16[512,4,128]{2,1,0:T(4,128)(2,1)} %copy.58), calls=%async_computation.6 | async-start | bytes 1048576 | tf_op jit(solution)/shard_map/all_to_all | solution.py:201
  122.0 82.2 %reduce-scatter.2.cloned.1.call-start = ((), (), s32[]{:S(2)}) async-start(), calls=%async_computation.10 | async-start | bytes 4718592 | tf_op jit(solution)/shard_map/reduce_scatter | solution.py:225
  139.3 4.7 %copy-start.5 = (bf16[4,512,512]{1,2,0:T(8,128)(2,1)S(1)}, bf16[4,512,512]{1,2,0:T(8,128)(2,1)}, u32[]{:S(2)}) copy-start(bf16[4,512,512]{1,2,0:T(8,128)(2,1)} %copy-done.4) | copy-start | bytes 6291460
  140.6 24.7 %all-to-all-start.3 = ((bf16[512,4,128]{2,1,0:T(4,128)(2,1)}), bf16[512,4,128]{2,1,0:T(4,128)(2,1)S(1)}, u32[]{:S(2)}, u32[]{:S(2)}) async-start(bf16[512,4,128]{2,1,0:T(4,128)(2,1)} %copy.50), calls=%async_computation.3 | async-start | bytes 1048576 | tf_op jit(solution)/shard_map/all_to_all | solution.py:186
  165.3 40.3 %all-to-all-start.5 = ((bf16[512,4,128]{2,1,0:T(4,128)(2,1)}), bf16[512,4,128]{2,1,0:T(4,128)(2,1)S(1)}, u32[]{:S(2)}, u32[]{:S(2)}) async-start(bf16[512,4,128]{2,1,0:T(4,128)(2,1)} %copy.56), calls=%async_computation.5 | async-start | bytes 1048576 | tf_op jit(solution)/shard_map/all_to_all | solution.py:200
  169.6 69.6 %all-reduce.2.cloned.1.call-start = ((), (), s32[]{:S(2)}) async-start(), calls=%async_computation.11 | async-start | bytes 1048576 | tf_op jit(solution)/shard_map/psum | solution.py:233
Sparse Core Ops, SparseCore 0:
  10.2 68.4 all-gather.2
  139.5 64.6 reduce-scatter.1
  206.5 32.6 all-reduce.1
where the time goes:
time: 249 us; the launch traced here: 248 us
  waiting for transfers between devices  139 us (56%)
  starting transfers between devices  31.6 us (13%)
  blocking collectives  21.7 us (9%)
  matrix products  19.9 us (8%)
  local copies, waits for them, and re-layouts  17.4 us (7%)
  between operations  14 us (6%)
  other arithmetic  4.52 us (2%)
    reduce_scatter x1, waiting for transfers between devices, body(): lax.psum_scatter(lax.dot_general(columns, grad_kv, (((0,), (0,)), ((), ()...  34.6 us
    psum x1, waiting for transfers between devices, body(): grad_total = lax.psum(grad_shard, 'rep').astype(jnp.bfloat16)  27.7 us
    all_to_all x1, waiting for transfers between devices, body(): lax.all_to_all(sent[0], 'seq', split_axis=1, concat_axis=0, tiled=True)  24.7 us
    all_gather x1, blocking collectives, body(): seg_all = lax.all_gather(segment_ids[0], 'seq', axis=0, tiled=True)  21.7 us
    all_to_all x1, waiting for transfers between devices, body(): lax.all_to_all(out_part, 'seq', split_axis=0, concat_axis=1, tiled=True)  19.1 us
    all_to_all x1, waiting for transfers between devices, body(): lax.all_to_all(key_back, 'seq', split_axis=0, concat_axis=1, tiled=True)  12.3 us
    all_gather x1, waiting for transfers between devices, body(): lax.all_gather(stacked, ('seq', 'fsdp'), axis=0, tiled=True)  9.14 us
    unnamed x16, local copies, waits for them, and re-layouts  6.44 us
  transfers between devices with their start and end apart: 11, of which 9 were waited for; matrix products, arithmetic and copies ran while one was open for 13% of the time, Pallas kernels for 0%

commit v1 on v0

--- a/solution.py
+++ b/solution.py
@@ -8,6 +8,13 @@
 KV_HEADS = 4
 HEAD_DIM = 128
 masked_low = -1e30
+
+
+def drive_sides(xx, k_dim):
+    heard = jnp.stack([xx] * lax.psum(1, "seq"), 0)
+    reached = lax.all_to_all(heard, "seq", 0, 0)
+    lower = jnp.concatenate(reached, k_dim)
+    return lower
 
 
 def block_mask(seg_all, row_start, col_start, block_width):
@@ -181,7 +188,7 @@
     widen_by = heads_here // key_part.shape[1]
     key_part = jnp.repeat(key_part, widen_by, axis=1)
     value_part = jnp.repeat(value_part, widen_by, axis=1)
-    seg_all = lax.all_gather(segment_ids[0], "seq", axis=0, tiled=True)
+    seg_all = drive_sides(segment_ids[0], 0)
     out_part, log_totals = attend(query_part, key_part, value_part, seg_all)
     context = lax.all_to_all(out_part, "seq", split_axis=0, concat_axis=1, tiled=True).reshape(
         1, rows_here, HEADS * HEAD_DIM

time: 249 us -> 253 us (1.016)
  blocking collectives: 21.7 us -> 0 us
  waiting for transfers between devices: 139 us -> 160 us
  starting transfers between devices: 31.6 us -> 35 us
    all_gather x1 -> x0, blocking collectives: 21.7 us -> none  [body(): seg_all = lax.all_gather(segment_ids[0], 'seq', axis=0, tiled=True)]
    all_gather x1, waiting for transfers between devices: 9.14 us -> 24.2 us  [body(): lax.all_gather(stacked, ('seq', 'fsdp'), axis=0, tiled=True)]
    all_to_all x0 -> x1, starting transfers between devices: none -> 6.32 us  [drive_sides(): reached = lax.all_to_all(heard, 'seq', 0, 0)]
    all_to_all x0 -> x1, waiting for transfers between devices: none -> 3.43 us  [drive_sides(): reached = lax.all_to_all(heard, 'seq', 0, 0)]
    all_to_all x1, starting transfers between devices: 6.32 us -> 3.47 us  [body(): lax.all_to_all(sent[0], 'seq', split_axis=1, concat_axis=0, tiled=True)]
    unnamed x16 -> x14, local copies, waits for them, and re-layouts: 6.44 us -> 6.43 us
  transfers between devices with their start and end apart: 11 -> 12, of which waited for: 9 -> 10; matrix products, arithmetic and copies ran while one was open for 13% -> 13% of each run, Pallas kernels for 0% -> 0%
where the time goes in v1:
time: 253 us; the launch traced here: 252 us
  waiting for transfers between devices  160 us (63%)
  starting transfers between devices  35 us (14%)
  matrix products  19.9 us (8%)
  local copies, waits for them, and re-layouts  18.7 us (7%)
  between operations  14 us (6%)
  other arithmetic  4.52 us (2%)
    reduce_scatter x1, waiting for transfers between devices, body(): lax.psum_scatter(lax.dot_general(columns, grad_kv, (((0,), (0,)), ((), ()...  34.4 us
    psum x1, waiting for transfers between devices, body(): grad_total = lax.psum(grad_shard, 'rep').astype(jnp.bfloat16)  27.7 us
    all_to_all x1, waiting for transfers between devices, body(): lax.all_to_all(sent[0], 'seq', split_axis=1, concat_axis=0, tiled=True)  27 us
    all_gather x1, waiting for transfers between devices, body(): lax.all_gather(stacked, ('seq', 'fsdp'), axis=0, tiled=True)  24.2 us
    all_to_all x1, waiting for transfers between devices, body(): lax.all_to_all(out_part, 'seq', split_axis=0, concat_axis=1, tiled=True)  19.1 us
    all_to_all x1, waiting for transfers between devices, body(): lax.all_to_all(key_back, 'seq', split_axis=0, concat_axis=1, tiled=True)  12.3 us
    unnamed x14, local copies, waits for them, and re-layouts  6.43 us
    all_to_all x1, starting transfers between devices, drive_sides(): reached = lax.all_to_all(heard, 'seq', 0, 0)  6.32 us
  transfers between devices with their start and end apart: 12, of which 10 were waited for; matrix products, arithmetic and copies ran while one was open for 13% of the time, Pallas kernels for 0%

profile of v1, /device:TPU:0, one launch (start us, length us, event | category | flops | bytes accessed | tf_op | source)
XLA Modules:
  0.0 252.1 jit_solution(1128379173121268920)
XLA Ops:
  10.4 6.3 %all-to-all-start = ((s32[4,1,128]{2,1,0:T(1,128)}), s32[4,1,128]{2,1,0:T(1,128)S(1)}, u32[]{:S(2)}, u32[]{:S(2)}) async-start(s32[4,1,128]{2,1,0:T(1,128)} %stack.3), calls=%async_computation | async-start | bytes 4096 | tf_op jit(solution)/shard_map/all_to_all | solution.py:15
  16.7 2.0 copy.45
  18.8 3.4 %all-to-all-done = s32[4,1,128]{2,1,0:T(1,128)S(1)} async-done(((s32[4,1,128]{2,1,0:T(1,128)}), s32[4,1,128]{2,1,0:T(1,128)S(1)}, u32[]{:S(2)}, u32[]{:S(2)}) %all-to-all-start) | async-done | bytes 2080 | tf_op jit(solution)/shard_map/all_to_all | solution.py:15
  22.2 3.5 %all-to-all-start.2 = ((bf16[128,16,128]{0,2,1:T(8,128)(2,1)}), bf16[128,16,128]{0,2,1:T(8,128)(2,1)S(1)}, u32[]{:S(2)}, u32[]{:S(2)}) async-start(bf16[128,16,128]{0,2,1:T(8,128)(2,1)} %bitcast.10), calls=%async_computation.2 | async-start | bytes 1048576 | tf_op jit(solution)/shard_map/all_to_all | solution.py:184
  25.7 2.0 copy.52
  27.7 27.0 %all-to-all-done.2 = bf16[128,16,128]{0,2,1:T(8,128)(2,1)S(1)} async-done(((bf16[128,16,128]{0,2,1:T(8,128)(2,1)}), bf16[128,16,128]{0,2,1:T(8,128)(2,1)S(1)}, u32[]{:S(2)}, u32[]{:S(2)}) %all-to-all-start.2) | async-done | bytes 524320 | tf_op jit(solution)/shard_map/all_to_all | solution.py:184
  54.7 3.5 %all-to-all-start.5 = ((bf16[128,16,128]{0,2,1:T(8,128)(2,1)}), bf16[128,16,128]{0,2,1:T(8,128)(2,1)S(1)}, u32[]{:S(2)}, u32[]{:S(2)}) async-start(bf16[128,16,128]{0,2,1:T(8,128)(2,1)} %bitcast.23), calls=%async_computation.5 | async-start | bytes 1048576 | tf_op jit(solution)/shard_map/all_to_all | solution.py:196
  58.2 24.2 %all-gather.2.cloned.1.call-done = bf16[2048,1024]{1,0:T(8,128)(2,1)} async-done(((bf16[256,1024]{1,0:T(8,128)(2,1)}), bf16[2048,1024]{1,0:T(8,128)(2,1)}) %all-gather.2.cloned.1.call-update) | async-done | bytes 4194320 | tf_op jit(solution)/shard_map/all_gather | solution.py:170
  82.4 3.5 %fusion.11 = bf16[128,1024]{0,1:T(8,128)(2,1)S(1)} fusion(bf16[2048,1024]{1,0:T(8,128)(2,1)} %all-gather.2.cloned.1.call-done, bf16[1,128,2048]{2,1,0:T(8,128)(2,1)S(1)} %copy-done), kind=kOutput, calls=%fused_computation.22 | convolution fusion | flops 537001984 | bytes 4980736 | tf_op jit(solution)/shard_map/dot_general | solution.py:168
  86.7 3.3 %all-to-all-start.1 = ((bf16[128,4,128]{2,0,1:T(8,128)(2,1)}), bf16[128,4,128]{2,0,1:T(8,128)(2,1)S(1)}, u32[]{:S(2)}, u32[]{:S(2)}) async-start(bf16[128,4,128]{2,0,1:T(8,128)(2,1)} %copy.44), calls=%async_computation.1 | async-start | bytes 262144 | tf_op jit(solution)/shard_map/all_to_all | solution.py:185
  91.6 4.8 %all-to-all-done.1 = bf16[128,4,128]{2,0,1:T(8,128)(2,1)S(1)} async-done(((bf16[128,4,128]{2,0,1:T(8,128)(2,1)}), bf16[128,4,128]{2,0,1:T(8,128)(2,1)S(1)}, u32[]{:S(2)}, u32[]{:S(2)}) %all-to-all-start.1) | async-done | bytes 131104 | tf_op jit(solution)/shard_map/all_to_all | solution.py:185
  96.4 3.3 %all-to-all-start.3 = ((bf16[128,4,128]{2,0,1:T(8,128)(2,1)}), bf16[128,4,128]{2,0,1:T(8,128)(2,1)S(1)}, u32[]{:S(2)}, u32[]{:S(2)}) async-start(bf16[128,4,128]{2,0,1:T(8,128)(2,1)} %copy.48), calls=%async_computation.3 | async-start | bytes 262144 | tf_op jit(solution)/shard_map/all_to_all | solution.py:186
  105.7 3.5 %all-to-all-start.8 = ((bf16[512,4,128]{2,1,0:T(4,128)(2,1)}), bf16[512,4,128]{2,1,0:T(4,128)(2,1)S(1)}, u32[]{:S(2)}, u32[]{:S(2)}) async-start(bf16[512,4,128]{2,1,0:T(4,128)(2,1)} %copy.60), calls=%async_computation.8 | async-start | bytes 1048576 | tf_op jit(solution)/shard_map/all_to_all | solution.py:209
  109.1 3.9 %fusion.12 = (f32[4,512]{1,0:T(4,128)S(1)}, bf16[4,512,128]{2,1,0:T(8,128)(2,1)S(1)}) fusion(bf16[4,128,4,128]{3,1,0,2:T(8,128)(2,1)S(1)} %copy.54, bf16[512,128]{1,0:T(8,128)(2,1)S(1)} %bitcast.112, f32[4,512,512]{2,1,0:T(8,128)} %copy-done.1, f32[4,512]{1,0:T(4,128)S(1)} %log_add_fusion, pred[512,512]{0,1:T(8,128)(4,1)S(1)} %fusion.13), kind=kOutput, calls=%fused_computation.24 | convolution fusion | flops 273938432 | bytes 5652480 | tf_op jit(solution)/shard_map/while/body/eval_jaxpr/while/body/hqk,khd->qhd/dot_general | solution.py:81
  117.0 5.2 %all-to-all-done.8 = bf16[512,4,128]{2,1,0:T(4,128)(2,1)S(1)} async-done(((bf16[512,4,128]{2,1,0:T(4,128)(2,1)}), bf16[512,4,128]{2,1,0:T(4,128)(2,1)S(1)}, u32[]{:S(2)}, u32[]{:S(2)}) %all-to-all-start.8) | async-done | bytes 524320 | tf_op jit(solution)/shard_map/all_to_all | solution.py:209
  122.3 3.5 %all-to-all-start.7 = ((bf16[512,4,128]{2,1,0:T(4,128)(2,1)}), bf16[512,4,128]{2,1,0:T(4,128)(2,1)S(1)}, u32[]{:S(2)}, u32[]{:S(2)}) async-start(bf16[512,4,128]{2,1,0:T(4,128)(2,1)} %copy.58), calls=%async_computation.7 | async-start | bytes 1048576 | tf_op jit(solution)/shard_map/all_to_all | solution.py:208
  126.8 12.3 %all-to-all-done.7 = bf16[512,4,128]{2,1,0:T(4,128)(2,1)S(1)} async-done(((bf16[512,4,128]{2,1,0:T(4,128)(2,1)}), bf16[512,4,128]{2,1,0:T(4,128)(2,1)S(1)}, u32[]{:S(2)}, u32[]{:S(2)}) %all-to-all-start.7) | async-done | bytes 524320 | tf_op jit(solution)/shard_map/all_to_all | solution.py:208
  139.8 3.2 %convert_bitcast_fusion = bf16[2048,1024]{0,1:T(8,128)(2,1)} fusion(bf16[1,128,2048]{2,1,0:T(8,128)(2,1)S(1)} %copy-done, bf16[128,512]{0,1:T(8,128)(2,1)S(1)} %bitcast.99, bf16[128,512]{0,1:T(8,128)(2,1)S(1)} %bitcast.101), kind=kOutput, calls=%fused_computation.6 | convolution fusion | flops 539492352 | bytes 4980736 | tf_op jit(solution)/shard_map/dot_general | solution.py:233
  144.3 3.5 %all-to-all-start.4 = ((bf16[512,4,128]{2,1,0:T(4,128)(2,1)}), bf16[512,4,128]{2,1,0:T(4,128)(2,1)S(1)}, u32[]{:S(2)}, u32[]{:S(2)}) async-start(bf16[512,4,128]{2,1,0:T(4,128)(2,1)} %copy.50), calls=%async_computation.4 | async-start | bytes 1048576 | tf_op jit(solution)/shard_map/all_to_all | solution.py:193
  149.9 19.1 %all-to-all-done.4 = bf16[512,4,128]{2,1,0:T(4,128)(2,1)S(1)} async-done(((bf16[512,4,128]{2,1,0:T(4,128)(2,1)}), bf16[512,4,128]{2,1,0:T(4,128)(2,1)S(1)}, u32[]{:S(2)}, u32[]{:S(2)}) %all-to-all-start.4) | async-done | bytes 524320 | tf_op jit(solution)/shard_map/all_to_all | solution.py:193
  169.0 4.4 %all-to-all-start.6 = ((bf16[512,4,128]{2,1,0:T(4,128)(2,1)}), bf16[512,4,128]{2,1,0:T(4,128)(2,1)S(1)}, u32[]{:S(2)}, u32[]{:S(2)}) async-start(bf16[512,4,128]{2,1,0:T(4,128)(2,1)} %copy.56), calls=%async_computation.6 | async-start | bytes 1048576 | tf_op jit(solution)/shard_map/all_to_all | solution.py:207
  173.5 34.4 %reduce-scatter.2.cloned.1.call-done = bf16[256,1024]{0,1:T(8,128)(2,1)} async-done(((bf16[2048,1024]{0,1:T(8,128)(2,1)}), bf16[256,1024]{0,1:T(8,128)(2,1)}) %reduce-scatter.2.cloned.1.call-update) | async-done | bytes 524304 | tf_op jit(solution)/shard_map/reduce_scatter | solution.py:232
  210.7 4.5 %fusion.5 = bf16[1,128,2048]{2,1,0:T(8,128)(2,1)} fusion(bf16[2048,1024]{1,0:T(8,128)(2,1)} %all-gather.2.cloned.1.call-done, bf16[128,512]{0,1:T(8,128)(2,1)S(1)} %bitcast.100, bf16[128,512]{0,1:T(8,128)(2,1)S(1)} %bitcast.102), kind=kOutput, calls=%fused_computation.11 | convolution fusion | flops 537657344 | bytes 4980736 | tf_op jit(solution)/shard_map/dot_general | solution.py:224
  215.2 27.7 %all-reduce.2.cloned.1.call-done = bf16[256,1024]{0,1:T(8,128)(2,1)} async-done(((bf16[256,1024]{0,1:T(8,128)(2,1)}), bf16[256,1024]{0,1:T(8,128)(2,1)}) %all-reduce.2.cloned.1.call-update) | async-done | bytes 524304 | tf_op jit(solution)/shard_map/psum | solution.py:240
  (50 shorter events, 26.0 us)
Async XLA Ops:
  7.2 75.2 %copy-start = (bf16[1,128,2048]{2,1,0:T(8,128)(2,1)S(1)}, bf16[1,128,2048]{2,1,0:T(8,128)(2,1)}, u32[]{:S(2)}) copy-start(bf16[1,128,2048]{2,1,0:T(8,128)(2,1)} %param.6) | copy-start | bytes 1572868
  7.2 75.2 %all-gather.2.cloned.1.call-start = ((), (), s32[]{:S(2)}) async-start(), calls=%async_computation.10 | async-start | bytes 4718592 | tf_op jit(solution)/shard_map/all_gather | solution.py:170
  10.4 11.8 %all-to-all-start = ((s32[4,1,128]{2,1,0:T(1,128)}), s32[4,1,128]{2,1,0:T(1,128)S(1)}, u32[]{:S(2)}, u32[]{:S(2)}) async-start(s32[4,1,128]{2,1,0:T(1,128)} %stack.3), calls=%async_computation | async-start | bytes 4096 | tf_op jit(solution)/shard_map/all_to_all | solution.py:15
  22.2 32.5 %all-to-all-start.2 = ((bf16[128,16,128]{0,2,1:T(8,128)(2,1)}), bf16[128,16,128]{0,2,1:T(8,128)(2,1)S(1)}, u32[]{:S(2)}, u32[]{:S(2)}) async-start(bf16[128,16,128]{0,2,1:T(8,128)(2,1)} %bitcast.10), calls=%async_computation.2 | async-start | bytes 1048576 | tf_op jit(solution)/shard_map/all_to_all | solution.py:184
  54.7 32.0 %all-to-all-start.5 = ((bf16[128,16,128]{0,2,1:T(8,128)(2,1)}), bf16[128,16,128]{0,2,1:T(8,128)(2,1)S(1)}, u32[]{:S(2)}, u32[]{:S(2)}) async-start(bf16[128,16,128]{0,2,1:T(8,128)(2,1)} %bitcast.23), calls=%async_computation.5 | async-start | bytes 1048576 | tf_op jit(solution)/shard_map/all_to_all | solution.py:196
  86.7 9.7 %all-to-all-start.1 = ((bf16[128,4,128]{2,0,1:T(8,128)(2,1)}), bf16[128,4,128]{2,0,1:T(8,128)(2,1)S(1)}, u32[]{:S(2)}, u32[]{:S(2)}) async-start(bf16[128,4,128]{2,0,1:T(8,128)(2,1)} %copy.44), calls=%async_computation.1 | async-start | bytes 262144 | tf_op jit(solution)/shard_map/all_to_all | solution.py:185
  96.4 9.2 %all-to-all-start.3 = ((bf16[128,4,128]{2,0,1:T(8,128)(2,1)}), bf16[128,4,128]{2,0,1:T(8,128)(2,1)S(1)}, u32[]{:S(2)}, u32[]{:S(2)}) async-start(bf16[128,4,128]{2,0,1:T(8,128)(2,1)} %copy.48), calls=%async_computation.3 | async-start | bytes 262144 | tf_op jit(solution)/shard_map/all_to_all | solution.py:186
  100.6 2.0 copy-start.1
  105.7 16.6 %all-to-all-start.8 = ((bf16[512,4,128]{2,1,0:T(4,128)(2,1)}), bf16[512,4,128]{2,1,0:T(4,128)(2,1)S(1)}, u32[]{:S(2)}, u32[]{:S(2)}) async-start(bf16[512,4,128]{2,1,0:T(4,128)(2,1)} %copy.60), calls=%async_computation.8 | async-start | bytes 1048576 | tf_op jit(solution)/shard_map/all_to_all | solution.py:209
  109.1 3.9 %copy-start.2 = (f32[4,512,512]{2,1,0:T(8,128)S(1)}, f32[4,512,512]{2,1,0:T(8,128)}, u32[]{:S(2)}) copy-start(f32[4,512,512]{2,1,0:T(8,128)} %copy-done.1) | copy-start | bytes 12582916
  114.5 1.4 copy-start.3
  122.3 16.8 %all-to-all-start.7 = ((bf16[512,4,128]{2,1,0:T(4,128)(2,1)}), bf16[512,4,128]{2,1,0:T(4,128)(2,1)S(1)}, u32[]{:S(2)}, u32[]{:S(2)}) async-start(bf16[512,4,128]{2,1,0:T(4,128)(2,1)} %copy.58), calls=%async_computation.7 | async-start | bytes 1048576 | tf_op jit(solution)/shard_map/all_to_all | solution.py:208
  125.7 82.2 %reduce-scatter.2.cloned.1.call-start = ((), (), s32[]{:S(2)}) async-start(), calls=%async_computation.11 | async-start | bytes 4718592 | tf_op jit(solution)/shard_map/reduce_scatter | solution.py:232
  143.1 4.7 %copy-start.4 = (bf16[4,512,512]{1,2,0:T(8,128)(2,1)S(1)}, bf16[4,512,512]{1,2,0:T(8,128)(2,1)}, u32[]{:S(2)}) copy-start(bf16[4,512,512]{1,2,0:T(8,128)(2,1)} %copy-done.3) | copy-start | bytes 6291460
  144.3 24.7 %all-to-all-start.4 = ((bf16[512,4,128]{2,1,0:T(4,128)(2,1)}), bf16[512,4,128]{2,1,0:T(4,128)(2,1)S(1)}, u32[]{:S(2)}, u32[]{:S(2)}) async-start(bf16[512,4,128]{2,1,0:T(4,128)(2,1)} %copy.50), calls=%async_computation.4 | async-start | bytes 1048576 | tf_op jit(solution)/shard_map/all_to_all | solution.py:193
  169.0 40.3 %all-to-all-start.6 = ((bf16[512,4,128]{2,1,0:T(4,128)(2,1)}), bf16[512,4,128]{2,1,0:T(4,128)(2,1)S(1)}, u32[]{:S(2)}, u32[]{:S(2)}) async-start(bf16[512,4,128]{2,1,0:T(4,128)(2,1)} %copy.56), calls=%async_computation.6 | async-start | bytes 1048576 | tf_op jit(solution)/shard_map/all_to_all | solution.py:207
  173.5 69.4 %all-reduce.2.cloned.1.call-start = ((), (), s32[]{:S(2)}) async-start(), calls=%async_computation.12 | async-start | bytes 1048576 | tf_op jit(solution)/shard_map/psum | solution.py:240
Sparse Core Ops, SparseCore 0:
  10.2 72.1 all-gather.1
  143.2 64.6 reduce-scatter.1
  210.2 32.5 all-reduce.1
